TPU v7x, 32 devices: a whole 2x2x4 slice. The times are simulated.
32 devices in a mesh: replica: 8 (over z, x), shard: 4 (over y, core).
Axes of the slice: x: 2, y: 2, z: 4, core: 2. Of those that a mesh axis runs over, the one named last changes fastest.
Arguments:
- tokens: bfloat16 [8192, 768], P(('replica', 'shard')), may hold values from -6 to 6
- pass_ids: int32 [8192], P(('replica', 'shard')), may hold values from 0 to 4
- seg_ids: int32 [8192], P('replica'), may hold values from 0 to 19, never falling along the last dimension, each value on 1 to 800 neighbouring positions
- cotangent: bfloat16 [8192, 768], P(('replica', 'shard')), may hold values from -6 to 6
- pass_table: bfloat16 [768, 5], P('shard'), may hold values from -3 to 3
- norm1_gain: bfloat16 [768], P('shard'), may hold values from 0.5 to 1.5
- norm1_bias: bfloat16 [768], P('shard'), may hold values from -2 to 2
- qkv_weight: bfloat16 [768, 2304], P('shard'), may hold values from -0.21875 to 0.21875
- out_weight: bfloat16 [768, 768], P('shard'), may hold values from -0.875 to 0.875
- out_bias: bfloat16 [768], P('shard'), may hold values from -2 to 2
- norm2_gain: bfloat16 [768], P('shard'), may hold values from 0.5 to 1.5
- norm2_bias: bfloat16 [768], P('shard'), may hold values from -2 to 2
- up_weight: bfloat16 [768, 3072], P('shard'), may hold values from -0.21875 to 0.21875
- up_bias: bfloat16 [3072], P('shard'), may hold values from -3 to 3
- down_weight: bfloat16 [3072, 768], P('shard'), may hold values from -0.109375 to 0.109375
- down_bias: bfloat16 [768], P('shard'), may hold values from -2 to 2
Outputs:
- output: bfloat16 [8192, 768], P(('replica', 'shard'))
- tokens_grad: bfloat16 [8192, 768], P(('replica', 'shard'))
- pass_table_grad: float32 [768, 5], P('shard')
- norm1_gain_grad: float32 [768], P('shard')
- norm1_bias_grad: float32 [768], P('shard')
- qkv_weight_grad: float32 [768, 2304], P('shard')
- out_weight_grad: float32 [768, 768], P('shard')
- out_bias_grad: float32 [768], P('shard')
- norm2_gain_grad: float32 [768], P('shard')
- norm2_bias_grad: float32 [768], P('shard')
- up_weight_grad: float32 [768, 3072], P('shard')
- up_bias_grad: float32 [3072], P('shard')
- down_weight_grad: float32 [3072, 768], P('shard')
- down_bias_grad: float32 [768], P('shard')
All inputs are finite; a program needn't handle non-finite values.
Results may differ from a plain program's by a relative error of at most 0.014.
Values may be sent and summed in bfloat16 or wider, within the bound.
No kernel may reach another device: no remote copies, remote signals or barrier semaphores. Data moves between devices by JAX's collectives and lax.ppermute only.
A program may use at most 128 MiB of HBM per device.

v0:
```python
import jax
import jax.numpy as jnp
from jax import lax
from jax.sharding import PartitionSpec as P

H = 12
HD = 64


epsilon = 1e-05
score_scale = 0.125
masked_score = -1e30


def gelu_tanh(value):
    return jax.nn.gelu(value, approximate=True)


def norm_forward(values, gain, bias):
    centre = jnp.mean(values, -1, keepdims=True)
    centred = values - centre
    inverse = lax.rsqrt(jnp.mean(centred * centred, -1, keepdims=True) + epsilon)
    unit_rows = centred * inverse
    return (unit_rows * gain + bias, unit_rows, inverse)


def norm_backward(grad_rows, unit_rows, inverse, gain):
    scaled = grad_rows * gain
    back_rows = inverse * (
        scaled
        - jnp.mean(scaled, -1, keepdims=True)
        - unit_rows * jnp.mean(scaled * unit_rows, -1, keepdims=True)
    )
    return (back_rows, jnp.sum(grad_rows * unit_rows, 0), jnp.sum(grad_rows, 0))


def shards(
    tokens,
    pass_ids,
    seg_ids,
    cotangent,
    pass_table,
    norm1_gain,
    norm1_bias,
    qkv_weight,
    out_weight,
    out_bias,
    norm2_gain,
    norm2_bias,
    up_weight,
    up_bias,
    down_weight,
    down_bias,
):
    f32 = jnp.float32
    bf16 = jnp.bfloat16
    (
        pass_full,
        gain_one,
        bias_one,
        qkv_full,
        out_full,
        out_bias_full,
        gain_two,
        bias_two,
        up_full,
        up_bias_full,
        down_full,
        down_bias_full,
    ) = (
        lax.all_gather(pass_table, "shard", axis=0, tiled=True),
        lax.all_gather(norm1_gain, "shard", axis=0, tiled=True),
        lax.all_gather(norm1_bias, "shard", axis=0, tiled=True),
        lax.all_gather(qkv_weight, "shard", axis=0, tiled=True),
        lax.all_gather(out_weight, "shard", axis=0, tiled=True),
        lax.all_gather(out_bias, "shard", axis=0, tiled=True),
        lax.all_gather(norm2_gain, "shard", axis=0, tiled=True),
        lax.all_gather(norm2_bias, "shard", axis=0, tiled=True),
        lax.all_gather(up_weight, "shard", axis=0, tiled=True),
        lax.all_gather(up_bias, "shard", axis=0, tiled=True),
        lax.all_gather(down_weight, "shard", axis=0, tiled=True),
        lax.all_gather(down_bias, "shard", axis=0, tiled=True),
    )
    row_count = tokens.shape[0]
    width = tokens.shape[1]
    seq_rows = seg_ids.shape[0]
    span = min(row_count, 512)
    blocks = row_count // span
    shard_rank = lax.axis_index("shard")
    row_offset = shard_rank * row_count
    own_seg = lax.dynamic_slice_in_dim(seg_ids, row_offset, row_count)
    key_pos = jnp.arange(seq_rows)

    def visible_at(start_row):
        query_pos = row_offset + start_row + jnp.arange(span)
        return (seg_ids[None, :] == own_seg[:, None]) & (key_pos[None, :] <= query_pos[:, None])

    one_hot = (pass_ids[:, None] == jnp.arange(pass_full.shape[1])[None, :]).astype(f32)
    stream_in = tokens.astype(f32) + jnp.einsum(
        "rp,dp->rd", one_hot, pass_full.astype(f32), precision=lax.Precision.HIGHEST
    )
    normed_one, unit_one, inverse_one = norm_forward(
        stream_in, gain_one.astype(f32), bias_one.astype(f32)
    )
    normed_low = normed_one.astype(bf16)
    qkv_low = jnp.dot(normed_low, qkv_full, preferred_element_type=f32).astype(bf16)
    query_low = qkv_low[:, :width]
    kv_own = qkv_low[:, width:]
    kv_all = lax.all_gather(kv_own, "shard", axis=0, tiled=True)
    query_heads = query_low.reshape(row_count, H, HD).transpose(1, 0, 2)
    key_heads = kv_all[:, :width].reshape(seq_rows, H, HD).transpose(1, 0, 2)
    value_heads = kv_all[:, width:].reshape(seq_rows, H, HD).transpose(1, 0, 2)

    def head_forward(items):
        query_head, key_head, value_head = items

        def block_forward(block_index):
            start_row = block_index * span
            scores = (
                jnp.einsum("qd,kd->qk", query_head, key_head, preferred_element_type=f32)
                * score_scale
            )
            scores = jnp.where(visible_at(start_row), scores, masked_score)
            row_top = jnp.max(scores, -1, keepdims=True)
            exp_scores = jnp.exp(scores - row_top)
            row_total = jnp.sum(exp_scores, -1, keepdims=True)
            prob_low = (exp_scores / row_total).astype(bf16)
            context_block = jnp.dot(prob_low, value_head, preferred_element_type=f32)
            return (context_block, (row_top + jnp.log(row_total))[:, 0])

        return lax.map(block_forward, jnp.arange(blocks))

    context_heads, log_totals = lax.map(head_forward, (query_heads, key_heads, value_heads))
    context = context_heads.reshape(H, row_count, HD).transpose(1, 0, 2).reshape(row_count, width)
    context_low = context.astype(bf16)
    stream_mid = (
        stream_in
        + jnp.dot(context_low, out_full, preferred_element_type=f32)
        + out_bias_full.astype(f32)
    )
    normed_two, unit_two, inverse_two = norm_forward(
        stream_mid, gain_two.astype(f32), bias_two.astype(f32)
    )
    normed_low_two = normed_two.astype(bf16)
    pre_act = jnp.dot(normed_low_two, up_full, preferred_element_type=f32) + up_bias_full.astype(
        f32
    )
    activation, gelu_back = jax.vjp(gelu_tanh, pre_act)
    act_low = activation.astype(bf16)
    output = (
        stream_mid
        + jnp.dot(act_low, down_full, preferred_element_type=f32)
        + down_bias_full.astype(f32)
    ).astype(bf16)
    (
        pass_full,
        gain_one,
        bias_one,
        qkv_full,
        out_full,
        out_bias_full,
        gain_two,
        bias_two,
        up_full,
        up_bias_full,
        down_full,
        down_bias_full,
    ) = (
        lax.all_gather(pass_table, "shard", axis=0, tiled=True),
        lax.all_gather(norm1_gain, "shard", axis=0, tiled=True),
        lax.all_gather(norm1_bias, "shard", axis=0, tiled=True),
        lax.all_gather(qkv_weight, "shard", axis=0, tiled=True),
        lax.all_gather(out_weight, "shard", axis=0, tiled=True),
        lax.all_gather(out_bias, "shard", axis=0, tiled=True),
        lax.all_gather(norm2_gain, "shard", axis=0, tiled=True),
        lax.all_gather(norm2_bias, "shard", axis=0, tiled=True),
        lax.all_gather(up_weight, "shard", axis=0, tiled=True),
        lax.all_gather(up_bias, "shard", axis=0, tiled=True),
        lax.all_gather(down_weight, "shard", axis=0, tiled=True),
        lax.all_gather(down_bias, "shard", axis=0, tiled=True),
    )
    cotangent_f = cotangent.astype(f32)
    grad_down = jnp.einsum("rf,rd->fd", act_low, cotangent, preferred_element_type=f32)
    grad_down_bias = jnp.sum(cotangent_f, 0)
    act_grad = jnp.einsum("rd,fd->rf", cotangent, down_full, preferred_element_type=f32)
    pre_grad = gelu_back(act_grad)[0].astype(bf16)
    grad_up = jnp.einsum("rd,rf->df", normed_low_two, pre_grad, preferred_element_type=f32)
    grad_up_bias = jnp.sum(pre_grad.astype(f32), 0)
    n2_grad = jnp.einsum("rf,df->rd", pre_grad, up_full, preferred_element_type=f32)
    norm_back_two, grad_gain_two, grad_bias_two = norm_backward(
        n2_grad, unit_two, inverse_two, gain_two.astype(f32)
    )
    mid_grad = cotangent_f + norm_back_two
    branch_grad = mid_grad.astype(bf16)
    grad_out = jnp.einsum("rd,re->de", context_low, branch_grad, preferred_element_type=f32)
    grad_out_bias = jnp.sum(branch_grad.astype(f32), 0)
    context_grad = jnp.einsum(
        "re,de->rd", branch_grad, out_full, preferred_element_type=f32
    ).astype(bf16)
    grad_heads = context_grad.reshape(row_count, H, HD).transpose(1, 0, 2)

    def head_backward(items):
        query_head, key_head, value_head, grad_head, log_head = items

        def block_backward(carry, block_index):
            key_grad, value_grad = carry
            start_row = block_index * span
            scores = (
                jnp.einsum("qd,kd->qk", query_head, key_head, preferred_element_type=f32)
                * score_scale
            )
            probs_full = jnp.where(
                visible_at(start_row), jnp.exp(scores - log_head[block_index][:, None]), 0.0
            )
            prob_low = probs_full.astype(bf16)
            value_grad = value_grad + jnp.einsum(
                "qk,qd->kd", prob_low, grad_head, preferred_element_type=f32
            )
            prob_grad = jnp.einsum("qd,kd->qk", grad_head, value_head, preferred_element_type=f32)
            row_delta = jnp.sum(prob_grad * probs_full, -1, keepdims=True)
            score_grad = (probs_full * (prob_grad - row_delta)).astype(bf16)
            query_grad = jnp.dot(score_grad, key_head, preferred_element_type=f32) * score_scale
            key_grad = (
                key_grad
                + jnp.einsum("qk,qd->kd", score_grad, query_head, preferred_element_type=f32)
                * score_scale
            )
            return ((key_grad, value_grad), query_grad)

        zero_rows = jnp.zeros((seq_rows, HD), f32)
        (key_grad, value_grad), query_grad = lax.scan(
            block_backward, (zero_rows, zero_rows), jnp.arange(blocks)
        )
        return (query_grad, key_grad, value_grad)

    query_grads, key_grads, value_grads = lax.map(
        head_backward, (query_heads, key_heads, value_heads, grad_heads, log_totals)
    )
    query_flat = query_grads.reshape(H, row_count, HD).transpose(1, 0, 2).reshape(row_count, width)
    key_flat = key_grads.transpose(1, 0, 2).reshape(seq_rows, width)
    value_flat = value_grads.transpose(1, 0, 2).reshape(seq_rows, width)
    kv_grad = jnp.concatenate([key_flat, value_flat], 1)
    kv_total = lax.psum_scatter(
        kv_grad.astype(jnp.bfloat16), "shard", scatter_dimension=0, tiled=True
    ).astype(jnp.float32)
    qkv_grad = jnp.concatenate([query_flat, kv_total], 1).astype(bf16)
    grad_qkv = jnp.einsum("rd,re->de", normed_low, qkv_grad, preferred_element_type=f32)
    n1_grad = jnp.einsum("re,de->rd", qkv_grad, qkv_full, preferred_element_type=f32)
    norm_back_one, grad_gain_one, grad_bias_one = norm_backward(
        n1_grad, unit_one, inverse_one, gain_one.astype(f32)
    )
    input_grad = mid_grad + norm_back_one
    tokens_grad = input_grad.astype(bf16)
    grad_pass = jnp.einsum("rd,rp->dp", input_grad, one_hot, precision=lax.Precision.HIGHEST)
    owned_grads = (
        lax.psum_scatter(
            grad_pass.astype(jnp.bfloat16), "shard", scatter_dimension=0, tiled=True
        ).astype(jnp.float32),
        lax.psum_scatter(
            grad_gain_one.astype(jnp.bfloat16), "shard", scatter_dimension=0, tiled=True
        ).astype(jnp.float32),
        lax.psum_scatter(
            grad_bias_one.astype(jnp.bfloat16), "shard", scatter_dimension=0, tiled=True
        ).astype(jnp.float32),
        lax.psum_scatter(
            grad_qkv.astype(jnp.bfloat16), "shard", scatter_dimension=0, tiled=True
        ).astype(jnp.float32),
        lax.psum_scatter(
            grad_out.astype(jnp.bfloat16), "shard", scatter_dimension=0, tiled=True
        ).astype(jnp.float32),
        lax.psum_scatter(
            grad_out_bias.astype(jnp.bfloat16), "shard", scatter_dimension=0, tiled=True
        ).astype(jnp.float32),
        lax.psum_scatter(
            grad_gain_two.astype(jnp.bfloat16), "shard", scatter_dimension=0, tiled=True
        ).astype(jnp.float32),
        lax.psum_scatter(
            grad_bias_two.astype(jnp.bfloat16), "shard", scatter_dimension=0, tiled=True
        ).astype(jnp.float32),
        lax.psum_scatter(
            grad_up.astype(jnp.bfloat16), "shard", scatter_dimension=0, tiled=True
        ).astype(jnp.float32),
        lax.psum_scatter(
            grad_up_bias.astype(jnp.bfloat16), "shard", scatter_dimension=0, tiled=True
        ).astype(jnp.float32),
        lax.psum_scatter(
            grad_down.astype(jnp.bfloat16), "shard", scatter_dimension=0, tiled=True
        ).astype(jnp.float32),
        lax.psum_scatter(
            grad_down_bias.astype(jnp.bfloat16), "shard", scatter_dimension=0, tiled=True
        ).astype(jnp.float32),
    )
    final_grads = lax.psum(
        (
            owned_grads[0],
            owned_grads[1],
            owned_grads[2],
            owned_grads[3],
            owned_grads[4],
            owned_grads[5],
            owned_grads[6],
            owned_grads[7],
            owned_grads[8],
            owned_grads[9],
            owned_grads[10],
            owned_grads[11],
        ),
        "replica",
    )
    return (output, tokens_grad) + tuple(final_grads)


def solution(mesh):
    placed = (
        P(("replica", "shard"), None),
        P(("replica", "shard")),
        P("replica"),
        P(("replica", "shard"), None),
        P("shard", None),
        P("shard"),
        P("shard"),
        P("shard", None),
        P("shard", None),
        P("shard"),
        P("shard"),
        P("shard"),
        P("shard", None),
        P("shard"),
        P("shard", None),
        P("shard"),
    )
    return jax.shard_map(
        shards,
        mesh=mesh,
        in_specs=placed,
        out_specs=(
            P(("replica", "shard"), None),
            P(("replica", "shard"), None),
            P("shard", None),
            P("shard"),
            P("shard"),
            P("shard", None),
            P("shard", None),
            P("shard"),
            P("shard"),
            P("shard"),
            P("shard", None),
            P("shard"),
            P("shard", None),
            P("shard"),
        ),
        check_vma=False,
    )
```

profile of v0, /device:TPU:0, one launch (start us, length us, event | category | flops | bytes accessed | tf_op | source)
XLA Modules:
  0.0 812.4 jit_solution(7417632322748173883)
XLA Ops:
  8.7 6.4 all-gather
  21.4 12.8 %all-reduce.15 = (bf16[768]{0:T(1024)(128)(2,1)S(1)}, bf16[768]{0:T(1024)(128)(2,1)S(1)}, bf16[768]{0:T(1024)(128)(2,1)S(1)}, bf16[768]{0:T(1024)(128)(2,1)S(1)}, bf16[768]{0:T(1024)(128)(2,1)S(1)}) all-reduce(bf16[768]{0:T(1024)(128)(2,1)S(1)} %dynamic-update-slice.1, ...), channel_id=1, replica_groups=mesh['replica'=8,'shard'=4] {'shard'}, use_global_device_ids=true, to_apply=%add.1 | all-reduce | flops 3840 | bytes 15360
  35.8 7.5 all-gather.8.cloned.1.call-done
  43.3 3.2 convolution_convert_fusion.3
  49.3 5.3 all-gather.1
  57.2 25.2 %all-gather.16.cloned.1.call-done = bf16[3072,768]{1,0:T(8,128)(2,1)} async-done(((bf16[768,768]{1,0:T(8,128)(2,1)}), bf16[3072,768]{1,0:T(8,128)(2,1)}) %all-gather.16.cloned.1.call-update) | async-done | bytes 4718608 | tf_op jit(solution)/shard_map/all_gather | solution.py:81
  82.4 5.5 fusion.73
  87.8 25.3 %all-gather.10.cloned.1.call-done = bf16[1024,1536]{1,0:T(8,128)(2,1)} async-done(((bf16[256,1536]{1,0:T(8,128)(2,1)}), bf16[1024,1536]{1,0:T(8,128)(2,1)}) %all-gather.10.cloned.1.call-update) | async-done | bytes 3145744 | tf_op jit(solution)/shard_map/all_gather | solution.py:109
  113.1 3.2 fusion.69
  116.3 2.6 copy.48
  118.9 4.2 copy.51
  124.7 4.1 copy.52
  128.9 44.2 %while.45 = (s32[]{:T(128)}, bf16[12,1,256,64]{2,3,1,0:T(8,128)(2,1)S(1)}, f32[12,1,256]{2,1,0:T(1,128)}, s32[1024]{0:T(1024)S(1)}, s32[256]{0:T(256)S(1)}, /*in...) while((s32[]{:T(128)}, ...), condition=%wide.region_5.6_spmd.clone, body=%wide.region_2.5_spmd.clone.sunk | while | flops 69992448 | bytes 3820661 | solution.py:133
  175.3 8.6 %fusion.66 = (bf16[3072]{0:T(1024)(128)(2,1)}, bf16[256,3072]{1,0:T(8,128)(2,1)S(1)}, f32[256,3072]{1,0:T(8,128)}) fusion(f32[256,3072]{1,0:T(8,128)} %fusion.73, f32[3072]{0:T(1024)S(1)} %bitcast.156, bf16[768,3072]{1,0:T(8,128)(2,1)} %all-gather.14.cloned.1.call-done, f32[256,768]{1,0:T(8,128)S(1)} %get-tuple-element.595, ...), kind=kOutput, calls=%fused_computation.128 | convolution fusion | flops 1226241024 | bytes 13395968 | tf_op jit(solution)/shard_map/dot_general | solution.py:145
  184.0 2.1 multiply_reduce_fusion.1
  189.2 1.9 copy.53
  191.9 97.1 %while.46 = (s32[]{:T(128)}, bf16[12,1,256,64]{2,3,1,0:T(8,128)(2,1)}, bf16[12,1024,64]{1,2,0:T(8,128)(2,1)}, bf16[12,1024,64]{1,2,0:T(8,128)(2,1)}, s32[1024]{0...) while((s32[]{:T(128)}, ...), condition=%wide.region_12.13_spmd.clone, body=%wide.region_10.12_spmd.clone.sunk | while | flops 170999808 | bytes 9454733 | solution.py:236
  236.0 1.9 fusion.121
  289.0 3.9 pad_maximum_fusion
  294.7 36.3 %reduce-scatter.9.cloned.1.call-done = bf16[256,1536]{0,1:T(8,128)(2,1)} async-done(((bf16[1024,1536]{0,1:T(8,128)(2,1)}), bf16[256,1536]{0,1:T(8,128)(2,1)}) %reduce-scatter.9.cloned.1.call-update) | async-done | bytes 786448 | tf_op jit(solution)/shard_map/reduce_scatter | solution.py:243
  331.0 3.6 multiply_reduce_fusion.2
  337.1 5.2 convolution_convert_fusion.1
  343.3 6.4 convolution_convert_fusion
  350.9 3.0 convolution_convert_fusion.2
  355.5 4.6 reduce-scatter.13.cloned.1.call-done
  360.1 10.2 %all-reduce.14 = (bf16[768]{0:T(1024)(128)(2,1)S(1)}, bf16[768]{0:T(1024)(128)(2,1)S(1)}, bf16[768]{0:T(1024)(128)(2,1)S(1)}, bf16[768]{0:T(1024)(128)(2,1)S(1)}...) all-reduce(bf16[768]{0:T(1024)(128)(2,1)S(1)} %dynamic-update-slice, ...), channel_id=1, replica_groups=mesh['replica'=8,'shard'=4] {'shard'}, use_global_device_ids=true, to_apply=%add.5 | all-reduce | flops 8448 | bytes 33792
  370.9 6.0 fusion.57
  376.9 6.0 reduce-scatter.19.cloned.1.call-done
  383.8 49.5 %reduce-scatter.15.cloned.1.call-done = bf16[192,3072]{1,0:T(8,128)(2,1)} async-done(((bf16[768,3072]{1,0:T(8,128)(2,1)}), bf16[192,3072]{1,0:T(8,128)(2,1)}) %reduce-scatter.15.cloned.1.call-update) | async-done | bytes 1179664 | tf_op jit(solution)/shard_map/reduce_scatter | solution.py:280
  433.3 50.4 %reduce-scatter.17.cloned.1.call-done = bf16[768,768]{1,0:T(8,128)(2,1)} async-done(((bf16[3072,768]{1,0:T(8,128)(2,1)}), bf16[768,768]{1,0:T(8,128)(2,1)}) %reduce-scatter.17.cloned.1.call-update) | async-done | bytes 1179664 | tf_op jit(solution)/shard_map/reduce_scatter | solution.py:286
  483.7 43.1 %reduce-scatter.11.cloned.1.call-done = bf16[192,2304]{1,0:T(8,128)(2,1)} async-done(((bf16[768,2304]{1,0:T(8,128)(2,1)}), bf16[192,2304]{1,0:T(8,128)(2,1)}) %reduce-scatter.11.cloned.1.call-update) | async-done | bytes 884752 | tf_op jit(solution)/shard_map/reduce_scatter | solution.py:265
  526.8 279.0 %all-reduce.17 = (f32[192,5]{0,1:T(8,128)}, f32[192]{0:T(256)}, f32[192]{0:T(256)}, f32[192,2304]{1,0:T(8,128)}, f32[192,768]{1,0:T(8,128)}, /*index=5*/f32[192]...) all-reduce(bf16[192,5]{0,1:T(8,128)(2,1)S(1)} %copy.59, ...), channel_id=1, replica_groups=mesh['replica'=8,'shard'=4] {'replica'}, use_global_device_ids=true, to_apply=%region_17.18 | all-reduce | flops 1772352 | bytes 10637952 | tf_op jit(solution)/shard_map/psum | solution.py:293
  (308 shorter events, 168.7 us)
Async XLA Ops:
  7.2 36.2 %all-gather.8.cloned.1.call-start = ((), (), s32[]{:S(2)}) async-start(), calls=%async_computation.6 | async-start | bytes 4423680 | tf_op jit(solution)/shard_map/all_gather | solution.py:74
  7.9 74.5 %all-gather.16.cloned.1.call-start = ((), (), s32[]{:S(2)}) async-start(), calls=%async_computation.10 | async-start | bytes 5898240 | tf_op jit(solution)/shard_map/all_gather | solution.py:81
  8.7 104.4 %all-gather.10.cloned.1.call-start = ((), (), s32[]{:S(2)}) async-start(), calls=%async_computation.7 | async-start | bytes 3932160 | tf_op jit(solution)/shard_map/all_gather | solution.py:109
  35.6 10.9 %copy-start.8 = (f32[256]{0:T(256)}, f32[256]{0:T(256)S(1)}, u32[]{:S(2)}) copy-start(f32[256]{0:T(256)S(1)} %broadcast_multiply_fusion.5) | copy-start | bytes 3076
  35.8 7.5 copy-start.13
  46.5 2.8 copy-start.24
  46.5 35.9 %copy-start.1 = (bf16[256,768]{1,0:T(8,128)(2,1)S(1)}, bf16[256,768]{1,0:T(8,128)(2,1)}, u32[]{:S(2)}) copy-start(bf16[256,768]{1,0:T(8,128)(2,1)} %param.23) | copy-start | bytes 1179652
  47.5 125.6 %all-gather.12.cloned.1.call-start = ((), (), s32[]{:S(2)}) async-start(), calls=%async_computation.8 | async-start | bytes 1474560 | tf_op jit(solution)/shard_map/all_gather | solution.py:75
  48.1 127.2 %all-gather.14.cloned.1.call-start = ((), (), s32[]{:S(2)}) async-start(), calls=%async_computation.9 | async-start | bytes 5898240 | tf_op jit(solution)/shard_map/all_gather | solution.py:79
  48.7 282.4 %reduce-scatter.9.cloned.1.call-start = ((), (), s32[]{:S(2)}) async-start(), calls=%async_computation.11 | async-start | bytes 3932160 | tf_op jit(solution)/shard_map/reduce_scatter | solution.py:243
  124.7 4.2 copy-start.25
  124.7 4.2 copy-start.26
  128.9 44.3 %copy-start.12 = (f32[768]{0:T(1024)S(1)}, f32[768]{0:T(1024)}, u32[]{:S(2)}) copy-start(f32[768]{0:T(1024)} %convert_element_type.171) | copy-start | bytes 9220
  175.0 9.0 %copy-start.10 = (f32[256]{0:T(256)}, f32[256]{0:T(256)S(1)}, u32[]{:S(2)}) copy-start(f32[256]{0:T(256)S(1)} %broadcast_multiply_fusion.4) | copy-start | bytes 3076
  175.2 8.7 %copy-start.15 = (f32[256]{0:T(256)}, f32[256]{0:T(256)S(1)}, u32[]{:S(2)}) copy-start(f32[256]{0:T(256)S(1)} %add_rsqrt_fusion) | copy-start | bytes 3076
  175.3 8.7 %copy-start.27 = (bf16[768,3072]{1,0:T(8,128)(2,1)S(1)}, bf16[768,3072]{1,0:T(8,128)(2,1)}, u32[]{:S(2)}) copy-start(bf16[768,3072]{1,0:T(8,128)(2,1)} %all-gather.14.cloned.1.call-done) | copy-start | bytes 14155780
  292.9 38.2 %copy-start.5 = (bf16[12,1,256,64]{2,3,1,0:T(8,128)(2,1)S(1)}, bf16[12,1,256,64]{2,3,1,0:T(8,128)(2,1)}, u32[]{:S(2)}) copy-start(bf16[12,1,256,64]{2,3,1,0:T(8,128)(2,1)} %get-tuple-element.411) | copy-start | bytes 1179652
  292.9 38.2 %copy-start.9 = (f32[256]{0:T(256)S(1)}, f32[256]{0:T(256)}, u32[]{:S(2)}) copy-start(f32[256]{0:T(256)} %copy-done.8) | copy-start | bytes 3076
  292.9 38.2 %copy-start.14 = (f32[256]{0:T(256)S(1)}, f32[256]{0:T(256)}, u32[]{:S(2)}) copy-start(f32[256]{0:T(256)} %copy-done.13) | copy-start | bytes 3076
  292.9 67.2 %reduce-scatter.13.cloned.1.call-start = ((), (), s32[]{:S(2)}) async-start(), calls=%async_computation.13 | async-start | bytes 1474560 | tf_op jit(solution)/shard_map/reduce_scatter | solution.py:268
  294.5 88.5 %reduce-scatter.19.cloned.1.call-start = ((), (), s32[]{:S(2)}) async-start(), calls=%async_computation.16 | async-start | bytes 245760
  334.7 2.5 copy-start.11
  334.7 2.4 copy-start.16
  337.1 96.2 %reduce-scatter.15.cloned.1.call-start = ((), (), s32[]{:S(2)}) async-start(), calls=%async_computation.14 | async-start | bytes 5898240 | tf_op jit(solution)/shard_map/reduce_scatter | solution.py:280
  342.3 141.4 %reduce-scatter.17.cloned.1.call-start = ((), (), s32[]{:S(2)}) async-start(), calls=%async_computation.15 | async-start | bytes 5898240 | tf_op jit(solution)/shard_map/reduce_scatter | solution.py:286
  349.7 177.1 %reduce-scatter.11.cloned.1.call-start = ((), (), s32[]{:S(2)}) async-start(), calls=%async_computation.12 | async-start | bytes 4423680 | tf_op jit(solution)/shard_map/reduce_scatter | solution.py:265
  353.9 6.2 copy-start.18
  353.9 6.2 copy-start.19
  353.9 6.2 copy-start.20
  353.9 6.2 copy-start.22
  353.9 6.2 copy-start.23
  370.9 155.9 %copy-start.7 = (bf16[192,768]{1,0:T(8,128)(2,1)S(1)}, bf16[192,768]{1,0:T(8,128)(2,1)}, u32[]{:S(2)}) copy-start(bf16[192,768]{1,0:T(8,128)(2,1)} %reduce-scatter.13.cloned.1.call-done) | copy-start | bytes 884740
  (8 other events, 13.0 us)
Sparse Core Ops, SparseCore 0:
  9.6 33.7 all-gather.7
  44.9 37.4 all-gather.15
  84.5 28.5 all-gather.9
  114.5 17.5 all-gather.11
  133.5 37.4 all-gather.13
  293.0 37.9 reduce-scatter.8
  334.3 25.7 reduce-scatter.12
  363.1 19.7 reduce-scatter.18
  385.5 47.8 reduce-scatter.14
  435.9 47.8 reduce-scatter.16
  486.3 40.4 reduce-scatter.10
where the time goes:
time: 816 us; the launch traced here: 812 us
  blocking collectives  314 us (38%)
  waiting for transfers between devices  250 us (31%)
  matrix products  170 us (21%)
  local copies, waits for them, and re-layouts  46 us (6%)
  between operations  16.2 us (2%)
  other arithmetic  14.7 us (2%)
    psum x1, blocking collectives, shards(): lax.psum((owned_grads[0], owned_grads[1], owned_grads[2], owned_grads[3],...  279 us
    reduce_scatter x1, waiting for transfers between devices, shards(): lax.psum_scatter(grad_down.astype(jnp.bfloat16), 'shard', scatter_dimensi...  50.4 us
    reduce_scatter x1, waiting for transfers between devices, shards(): lax.psum_scatter(grad_up.astype(jnp.bfloat16), 'shard', scatter_dimension...  49.5 us
    reduce_scatter x1, waiting for transfers between devices, shards(): lax.psum_scatter(grad_qkv.astype(jnp.bfloat16), 'shard', scatter_dimensio...  43.1 us
    reduce_scatter x1, waiting for transfers between devices, shards(): lax.psum_scatter(kv_grad.astype(jnp.bfloat16), 'shard', scatter_dimension...  36.3 us
    all_gather x1, waiting for transfers between devices, shards(): kv_all = lax.all_gather(kv_own, 'shard', axis=0, tiled=True)  25.3 us
    all_gather x1, waiting for transfers between devices, shards(): lax.all_gather(down_weight, 'shard', axis=0, tiled=True)  25.2 us
    unnamed x2, blocking collectives  23 us
  transfers between devices with their start and end apart: 11, of which 9 were waited for; matrix products, arithmetic and copies ran while one was open for 14% of the time, Pallas kernels for 0%

commit v1 on v0

v1 whole, which is shorter than its diff:
```python
import functools

import jax
import jax.numpy as jnp
from jax import lax
from jax.experimental import pallas as pl
from jax.experimental.pallas import tpu as pltpu
from jax.sharding import PartitionSpec as P

HD = 64
epsilon = 1e-05
score_scale = 0.125
masked_score = -1e30
f32 = jnp.float32
bf16 = jnp.bfloat16

CORE = [(i, i ^ 1) for i in range(4)]
ROWY = [(i, i ^ 2) for i in range(4)]


def contract(left, right, ld, rd):
    return lax.dot_general(left, right, (((ld,), (rd,)), ((), ())), preferred_element_type=f32)


def unit_of(values):
    centred = values - jnp.mean(values, -1, keepdims=True)
    inverse = lax.rsqrt(jnp.mean(centred * centred, -1, keepdims=True) + epsilon)
    return centred * inverse, inverse


def norm_back(grad_rows, unit_rows, inverse, gain):
    scaled = grad_rows * gain
    return inverse * (
        scaled
        - jnp.mean(scaled, -1, keepdims=True)
        - unit_rows * jnp.mean(scaled * unit_rows, -1, keepdims=True)
    )


def vmem_call(body, outs, scratch=()):
    return pl.pallas_call(
        body,
        out_shape=[jax.ShapeDtypeStruct(s, d) for s, d in outs],
        out_specs=[pl.BlockSpec(memory_space=pltpu.VMEM)] * len(outs),
        scratch_shapes=[pltpu.VMEM(s, d) for s, d in scratch],
    )


def at_rows(index, size):
    return pl.ds(pl.multiple_of(index * size, size), size)


def front_body(rank_ref, segc_ref, segr_ref, b0, b1, b2, b3, w0, w1, w2, w3, wout_ref,
               send_ref, keep_ref, sin_ref, par_ref, qkv_ref, ctx_ref, lse_ref, nrm_ref, wq_ref, lse_s):
    rank = rank_ref[0]
    blocks = (b0, b1, b2, b3)
    rows, width = sin_ref.shape
    part = width // 4
    ext = [b[rows:rows + 16, 0:part].astype(f32) for b in blocks]
    cols = []
    for j in range(4):
        acc = jnp.zeros_like(ext[0])
        for k in range(4):
            acc = jnp.where((rank ^ k) == j, ext[k], acc)
        cols.append(acc)
    par = jnp.concatenate(cols, axis=1)
    par_ref[...] = par
    table = par[0:8].astype(bf16)
    gain, bias = par[5:6], par[6:7]
    for k in range(4):
        b = blocks[k]
        ids = b[rows + 11:rows + 12, 0:rows].astype(f32)
        one = (lax.broadcasted_iota(jnp.int32, (8, rows), 0).astype(f32) == ids).astype(bf16)
        x = b[0:rows].astype(f32) + contract(one, table, 0, 0)
        if k == 0:
            sin_ref[...] = x
        unit, _ = unit_of(x)
        nrm_ref[at_rows(rank ^ k, rows)] = (unit * gain + bias).astype(bf16)
    for k, w in enumerate((w0, w1, w2, w3)):
        wq_ref[at_rows(rank ^ k, part)] = w[...]
    qkv_ref[...] = jnp.dot(nrm_ref[...], wq_ref[...], preferred_element_type=f32).astype(bf16)
    heads = part // HD
    for h in range(heads):
        q = qkv_ref[:, h * HD:(h + 1) * HD] * jnp.asarray(score_scale, bf16)
        key = qkv_ref[:, part + h * HD:part + (h + 1) * HD]
        val = qkv_ref[:, 2 * part + h * HD:2 * part + (h + 1) * HD]
        for i in range(4):
            lo, nk = i * rows, (i + 1) * rows
            sc = contract(q[lo:nk], key[:nk], 1, 1)
            qpos = lo + lax.broadcasted_iota(jnp.int32, (rows, nk), 0)
            kpos = lax.broadcasted_iota(jnp.int32, (rows, nk), 1)
            seen = (segc_ref[lo:nk] == segr_ref[:, :nk]) & (kpos <= qpos)
            sc = jnp.where(seen, sc, masked_score)
            top = jnp.max(sc, -1, keepdims=True)
            e = jnp.exp(sc - top)
            total = jnp.sum(e, -1, keepdims=True)
            prob = (e * (1.0 / total)).astype(bf16)
            ctx_ref[lo:nk, h * HD:(h + 1) * HD] = jnp.dot(
                prob, val[:nk], preferred_element_type=f32).astype(bf16)
            lse_s[lo:nk, h:h + 1] = top + jnp.log(total)
    lse_ref[...] = lse_s[...].T[0:8]
    for i, k in enumerate((1, 3)):
        send_ref[i * rows:(i + 1) * rows] = jnp.dot(
            ctx_ref[at_rows(rank ^ k, rows)], wout_ref[...], preferred_element_type=f32).astype(bf16)
    for i, k in enumerate((0, 2)):
        keep_ref[i * rows:(i + 1) * rows] = jnp.dot(
            ctx_ref[at_rows(rank ^ k, rows)], wout_ref[...], preferred_element_type=f32)


def mid_body(sin_ref, par_ref, keep_ref, recv_ref, yrecv_ref, mid_ref, nrm_ref):
    mid = (sin_ref[...] + keep_ref[...] + recv_ref[...].astype(f32)
           + yrecv_ref[...].astype(f32) + par_ref[7:8])
    mid_ref[...] = mid
    unit, _ = unit_of(mid)
    nrm_ref[...] = (unit * par_ref[8:9] + par_ref[9:10]).astype(bf16)


def gelu_pair(v):
    c0, c1 = 0.7978845608028654, 0.044715
    sq = v * v
    t = jnp.tanh(c0 * v * (1.0 + c1 * sq))
    half = 0.5 * (1.0 + t)
    return v * half, half + 0.5 * v * (1.0 - t * t) * (c0 * (1.0 + 3.0 * c1 * sq))


def feed_body(rank_ref, n0, n1, n2, n3, c0, c1, c2, c3, u0, u1, u2, u3, ub_ref, dw_ref,
              send_ref, keep_ref, act_ref, pg_ref, wu_s):
    rank = rank_ref[0]
    rows, width = n0.shape
    part = width // 4
    for k, u in enumerate((u0, u1, u2, u3)):
        wu_s[at_rows(rank ^ k, part)] = u[...]
    for k, (n, c) in enumerate(((n0, c0), (n1, c1), (n2, c2), (n3, c3))):
        pre = jnp.dot(n[...], wu_s[...], preferred_element_type=f32) + ub_ref[...]
        act, slope = gelu_pair(pre)
        act_ref[k * rows:(k + 1) * rows] = act.astype(bf16)
        pg = (contract(c[...], dw_ref[...], 1, 1) * slope).astype(bf16)
        pg_ref[k * rows:(k + 1) * rows] = pg
        back = contract(pg, wu_s[...], 1, 1)
        i = k // 2
        if k % 2:
            send_ref[i * rows:(i + 1) * rows] = back.astype(bf16)
        else:
            keep_ref[i * rows:(i + 1) * rows] = back


def feed_grad_body(n0, n1, n2, n3, c0, c1, c2, c3, dw_ref, act_ref, pg_ref,
                   send_ref, keep_ref, gd_ref, gu_ref, small_ref):
    rows, width = n0.shape
    gd = jnp.zeros(gd_ref.shape, f32)
    gu = jnp.zeros(gu_ref.shape, f32)
    up_b = jnp.zeros((1, pg_ref.shape[1]), f32)
    down_b = jnp.zeros((1, width), f32)
    for k, (n, c) in enumerate(((n0, c0), (n1, c1), (n2, c2), (n3, c3))):
        act = act_ref[k * rows:(k + 1) * rows]
        pg = pg_ref[k * rows:(k + 1) * rows]
        out = jnp.dot(act, dw_ref[...], preferred_element_type=f32)
        i = k // 2
        if k % 2:
            send_ref[i * rows:(i + 1) * rows] = out.astype(bf16)
        else:
            keep_ref[i * rows:(i + 1) * rows] = out
        gd = gd + contract(act, c[...], 0, 0)
        gu = gu + contract(n[...], pg, 0, 0)
        up_b = up_b + jnp.sum(pg.astype(f32), 0, keepdims=True)
        down_b = down_b + jnp.sum(c[...].astype(f32), 0, keepdims=True)
    gd_ref[...] = gd.astype(bf16)
    gu_ref[...] = gu.astype(bf16)
    small_ref[0:1] = up_b
    small_ref[1:2] = down_b


def mid_back_body(mid_ref, par_ref, cot_ref, keep_ref, recv_ref, yrecv_ref,
                  grad_ref, branch_ref, small_ref):
    back = keep_ref[...] + recv_ref[...].astype(f32) + yrecv_ref[...].astype(f32)
    unit, inverse = unit_of(mid_ref[...])
    grad = cot_ref[...].astype(f32) + norm_back(back, unit, inverse, par_ref[8:9])
    grad_ref[...] = grad
    branch_ref[...] = grad.astype(bf16)
    small_ref[0:1] = jnp.sum(back * unit, 0, keepdims=True)
    small_ref[1:2] = jnp.sum(back, 0, keepdims=True)


def attn_back_body(rank_ref, segc_ref, segr_ref, g0, g1, g2, g3, qkv_ref, ctx_ref, lse_ref, nrm_ref,
                   wq_ref, wout_ref, send_ref, keep_ref, go_ref, gq_ref, small_ref, dctx_s, del_s, dq_s, dqkv_s):
    rank = rank_ref[0]
    rows, width = g0.shape
    part = width // 4
    total_rows = qkv_ref.shape[0]
    go = jnp.zeros(go_ref.shape, f32)
    ob = jnp.zeros((1, width), f32)
    for k, g in enumerate((g0, g1, g2, g3)):
        at = at_rows(rank ^ k, rows)
        dctx_s[at] = contract(g[...], wout_ref[...], 1, 1).astype(bf16)
        go = go + contract(ctx_ref[at], g[...], 0, 0)
        ob = ob + jnp.sum(g[...].astype(f32), 0, keepdims=True)
    go_ref[...] = go.astype(bf16)
    small_ref[0:1] = ob
    heads = part // HD
    prod = dctx_s[...].astype(f32) * ctx_ref[...].astype(f32)
    for h in range(heads):
        del_s[:, h:h + 1] = jnp.sum(prod[:, h * HD:(h + 1) * HD], -1, keepdims=True)
    delta = del_s[...].T
    for h in range(heads):
        q = qkv_ref[:, h * HD:(h + 1) * HD] * jnp.asarray(score_scale, bf16)
        key = qkv_ref[:, part + h * HD:part + (h + 1) * HD]
        val = qkv_ref[:, 2 * part + h * HD:2 * part + (h + 1) * HD]
        dctx = dctx_s[:, h * HD:(h + 1) * HD]
        for j in range(total_rows // rows):
            lo = j * rows
            hi = lo + rows
            nq = total_rows - lo
            sc = contract(key[lo:hi], q[lo:], 1, 1)
            kpos = lax.broadcasted_iota(jnp.int32, (rows, nq), 0)
            qpos = lax.broadcasted_iota(jnp.int32, (rows, nq), 1)
            seen = (segc_ref[lo:hi] == segr_ref[:, lo:]) & (kpos <= qpos)
            prob = jnp.where(seen, jnp.exp(sc - lse_ref[h:h + 1, lo:]), 0.0)
            dv = jnp.dot(prob.astype(bf16), dctx[lo:], preferred_element_type=f32)
            dprob = contract(val[lo:hi], dctx[lo:], 1, 1)
            ds = (prob * (dprob - delta[h:h + 1, lo:])).astype(bf16)
            dk = jnp.dot(ds, q[lo:], preferred_element_type=f32)
            dq = contract(ds, key[lo:hi], 0, 0)
            if j == 0:
                dq_s[...] = dq
            else:
                dq_s[lo:] += dq
            dqkv_s[lo:hi, part + h * HD:part + (h + 1) * HD] = dk.astype(bf16)
            dqkv_s[lo:hi, 2 * part + h * HD:2 * part + (h + 1) * HD] = dv.astype(bf16)
        dqkv_s[:, h * HD:(h + 1) * HD] = (dq_s[...] * score_scale).astype(bf16)
    for i, k in enumerate((1, 3)):
        send_ref[i * rows:(i + 1) * rows] = contract(
            dqkv_s[at_rows(rank ^ k, rows)], wq_ref[...], 1, 1).astype(bf16)
    for i, k in enumerate((0, 2)):
        keep_ref[i * rows:(i + 1) * rows] = contract(dqkv_s[at_rows(rank ^ k, rows)], wq_ref[...], 1, 1)
    gq_ref[...] = contract(nrm_ref[...], dqkv_s[...], 0, 0).astype(bf16)


def last_body(sin_ref, par_ref, ids_ref, grad_ref, keep_ref, recv_ref, yrecv_ref, tok_ref, small_ref):
    back = keep_ref[...] + recv_ref[...].astype(f32) + yrecv_ref[...].astype(f32)
    unit, inverse = unit_of(sin_ref[...])
    grad = grad_ref[...] + norm_back(back, unit, inverse, par_ref[5:6])
    tok_ref[...] = grad.astype(bf16)
    small_ref[5:6] = jnp.sum(back * unit, 0, keepdims=True)
    small_ref[6:7] = jnp.sum(back, 0, keepdims=True)
    rows = grad.shape[0]
    ids = ids_ref[rows + 11:rows + 12, 0:rows].astype(f32)
    one = (lax.broadcasted_iota(jnp.int32, (8, rows), 0).astype(f32) == ids).astype(f32)
    by_pass = lax.dot_general(one, grad, (((1,), (0,)), ((), ())), precision=lax.Precision.HIGHEST,
                              preferred_element_type=f32)
    small_ref[0:5] = by_pass[0:5]


def gather_rows(block):
    by_core = lax.ppermute(block, "shard", CORE)
    by_row = lax.ppermute(block, "shard", ROWY)
    both = lax.ppermute(by_row, "shard", CORE)
    return block, by_core, by_row, both


def swap_blocks(pick):
    far = lax.ppermute(jnp.stack([pick(2), pick(3)]), "shard", ROWY)
    near = lax.ppermute(pick(1), "shard", CORE)
    both = lax.ppermute(far[1], "shard", CORE)
    return pick(0), near, far[0], both


def scatter_sum(send, keep, rows):
    recv = lax.ppermute(send, "shard", CORE)
    onward = (keep[rows:] + recv[rows:].astype(f32)).astype(bf16)
    far = lax.ppermute(onward, "shard", ROWY)
    return keep[:rows], recv[:rows], far


def masks_of(count):
    masks, bit = [], 1
    while bit < count:
        masks.append(6 if bit == 4 else bit)
        bit *= 2
    return masks


def coordinate(replica, position):
    bit = (replica >> position) & 1
    if position == 1:
        bit = bit ^ ((replica >> 2) & 1)
    return bit


def plane_scatter(value, order, count, replica):
    masks = masks_of(count)
    for position in order:
        pairs = [(i, i ^ masks[position]) for i in range(count)]
        half = value.reshape((2, value.shape[0] // 2) + value.shape[1:])
        own = coordinate(replica, position)
        send = lax.dynamic_index_in_dim(half, 1 - own, 0, keepdims=False)
        keep = lax.dynamic_index_in_dim(half, own, 0, keepdims=False)
        got = lax.ppermute(send.astype(bf16), "replica", pairs)
        value = keep.astype(f32) + got.astype(f32)
    return value


def plane_gather(value, order, count, replica):
    masks = masks_of(count)
    value = value.astype(bf16)
    for position in reversed(order):
        pairs = [(i, i ^ masks[position]) for i in range(count)]
        own = coordinate(replica, position)
        got = lax.ppermute(value, "replica", pairs)
        first = jnp.where(own == 0, value, got)
        second = jnp.where(own == 0, got, value)
        value = jnp.concatenate([first, second], 0)
    return value


def plane_sum(value, order, count, replica):
    rows = value.shape[0]
    parts = value.reshape((count, rows // count) + value.shape[1:])
    piece = plane_scatter(parts, order, count, replica)
    return plane_gather(piece, order, count, replica).reshape(value.shape)


def plane_sum_columns(value, order, count, replica, rank):
    rows, cols = value.shape[0] // 4, value.shape[1]
    parts = value.reshape(4, count, rows // count, cols).transpose(1, 0, 2, 3)
    piece = plane_scatter(parts, order, count, replica)[0].astype(bf16)
    blocks = swap_blocks(lambda k: lax.dynamic_index_in_dim(piece, rank ^ k, 0, keepdims=False))
    stack = jnp.stack(blocks)
    natural = jnp.stack([lax.dynamic_index_in_dim(stack, rank ^ j, 0, keepdims=False) for j in range(4)])
    full = plane_gather(natural[None], order, count, replica)
    return full.transpose(0, 2, 1, 3).reshape(rows, 4, cols)


def shards(replicas, tokens, pass_ids, seg_ids, cotangent, pass_table, norm1_gain, norm1_bias, qkv_weight, out_weight,
           out_bias, norm2_gain, norm2_bias, up_weight, up_bias, down_weight, down_bias):
    rows, width = tokens.shape
    part = width // 4
    seq = seg_ids.shape[0]
    rank = lax.axis_index("shard")
    replica = lax.axis_index("replica")
    rank_s = rank.reshape(1).astype(jnp.int32)
    smem = pl.BlockSpec(memory_space=pltpu.SMEM)
    vmem = pl.BlockSpec(memory_space=pltpu.VMEM)

    def call(body, outs, scratch, *args, ranked=True):
        specs = [smem] * ranked + [vmem] * (len(args) - ranked)
        return pl.pallas_call(
            body,
            out_shape=[jax.ShapeDtypeStruct(s, d) for s, d in outs],
            in_specs=specs,
            out_specs=[vmem] * len(outs),
            scratch_shapes=[pltpu.VMEM(s, d) for s, d in scratch],
        )(*args)

    def row_of(vector):
        return jnp.pad(vector.astype(bf16), (0, width - vector.shape[0]))[None]

    extra = [jnp.pad(pass_table.T, ((0, 0), (0, width - part)))]
    extra += [row_of(v) for v in (norm1_gain, norm1_bias, out_bias, norm2_gain, norm2_bias, down_bias, pass_ids)]
    extra = jnp.concatenate(extra + [jnp.zeros((4, width), bf16)], 0)
    blocks = gather_rows(jnp.concatenate([tokens, extra], 0))

    columns = qkv_weight.reshape(part, 3, 4, part).transpose(2, 0, 1, 3).reshape(4, part, 3 * part)
    wq = swap_blocks(lambda k: lax.dynamic_index_in_dim(columns, rank ^ k, 0, keepdims=False))
    hidden = up_bias.shape[0]
    up_cols = up_weight.reshape(part, 4, hidden).transpose(1, 0, 2)
    wu = swap_blocks(lambda k: lax.dynamic_index_in_dim(up_cols, rank ^ k, 0, keepdims=False))
    cot = gather_rows(cotangent)

    segc, segr = seg_ids[:, None], seg_ids[None, :]
    send, keep, sin, par, qkv, ctx, lse, nrm, wq_full = call(
        front_body,
        [((2 * rows, width), bf16), ((2 * rows, width), f32), ((rows, width), f32), ((16, width), f32),
         ((seq, 3 * part), bf16), ((seq, part), bf16), ((8, seq), f32), ((seq, width), bf16), ((width, 3 * part), bf16)],
        [((seq, 128), f32)],
        rank_s, segc, segr, *blocks, *wq, out_weight)
    mid, nrm2 = call(mid_body, [((rows, width), f32), ((rows, width), bf16)], [],
                     sin, par, *scatter_sum(send, keep, rows), ranked=False)
    n2 = gather_rows(nrm2)
    send, keep, act, pg = call(
        feed_body,
        [((2 * rows, width), bf16), ((2 * rows, width), f32), ((seq, hidden), bf16), ((seq, hidden), bf16)],
        [((width, hidden), bf16)],
        rank_s, *n2, *cot, *wu, up_bias.astype(f32)[None], down_weight)
    back = scatter_sum(send, keep, rows)
    send, keep, grad_down, grad_up, small_feed = call(
        feed_grad_body,
        [((2 * rows, width), bf16), ((2 * rows, width), f32), ((hidden, width), bf16), ((width, hidden), bf16),
         ((8, width), f32)],
        [], *n2, *cot, down_weight, act, pg, ranked=False)
    mid_grad, branch, small_mid = call(
        mid_back_body, [((rows, width), f32), ((rows, width), bf16), ((8, width), f32)], [],
        mid, par, cotangent, *back, ranked=False)
    out_parts = scatter_sum(send, keep, rows)
    output = (mid + out_parts[0] + out_parts[1].astype(f32) + out_parts[2].astype(f32) + par[10:11]).astype(bf16)
    branches = gather_rows(branch)
    send, keep, grad_out, grad_qkv, small_attn = call(
        attn_back_body,
        [((2 * rows, width), bf16), ((2 * rows, width), f32), ((part, width), bf16), ((width, 3 * part), bf16),
         ((8, width), f32)],
        [((seq, part), bf16), ((seq, 128), f32), ((seq, HD), f32), ((seq, 3 * part), bf16)],
        rank_s, segc, segr, *branches, qkv, ctx, lse, nrm, wq_full, out_weight)
    tokens_grad, small_last = call(
        last_body, [((rows, width), bf16), ((8, width), f32)], [],
        sin, par, blocks[0], mid_grad, *scatter_sum(send, keep, rows), ranked=False)

    orders = [list(range(len(masks_of(replicas))))]
    for _ in range(2):
        orders.append(orders[-1][1:] + orders[-1][:1])
    final_down = plane_sum(grad_down, orders[0], replicas, replica).astype(f32)
    final_up = plane_sum_columns(grad_up, orders[1], replicas, replica, rank).astype(f32)
    final_up = final_up.reshape(part, 4 * hidden)
    final_out = plane_sum(grad_out, orders[2], replicas, replica).astype(f32)
    final_qkv = plane_sum_columns(grad_qkv, orders[0], replicas, replica, rank).astype(f32)
    final_qkv = final_qkv.reshape(part, 4, 3, part).transpose(0, 2, 1, 3).reshape(part, 12 * part)

    own = (lax.broadcasted_iota(jnp.int32, (4, 1), 0) == rank).astype(f32)
    up_slots = (own * small_feed[0:1]).reshape(4, hidden)
    complete = jnp.stack([small_feed[1], small_attn[0]]).reshape(2, 4, part) * own[None]
    packed = jnp.concatenate([
        small_last[0:7].reshape(7, 4, part), small_mid[0:2].reshape(2, 4, part), complete,
        up_slots.reshape(4, 4, part).transpose(1, 0, 2)], 0)
    packed = lax.psum(packed, ("replica", "shard"))
    mine = lax.dynamic_index_in_dim(packed, rank, 1, keepdims=False)
    return (
        output,
        tokens_grad,
        mine[0:5].T,
        mine[5],
        mine[6],
        final_qkv,
        final_out,
        mine[10],
        mine[7],
        mine[8],
        final_up,
        mine[11:15].reshape(hidden),
        final_down,
        mine[9],
    )


def solution(mesh):
    row = P(("replica", "shard"), None)
    flat = P(("replica", "shard"))
    w2, w1 = P("shard", None), P("shard")
    return jax.shard_map(
        functools.partial(shards, mesh.shape["replica"]),
        mesh=mesh,
        in_specs=(row, flat, P("replica"), row, w2, w1, w1, w2, w2, w1, w1, w1, w2, w1, w2, w1),
        out_specs=(row, row, w2, w1, w1, w2, w2, w1, w1, w1, w2, w1, w2, w1),
        check_vma=False,
    )
```

time: 816 us -> 344 us (0.42)
  blocking collectives: 314 us -> 43.9 us
  matrix products: 170 us -> 0 us
  waiting for transfers between devices: 250 us -> 99.1 us
  starting transfers between devices: 0.66 us -> 68 us
  Pallas kernels: 0 us -> 57.4 us
  between operations: 16.2 us -> 1.96 us
    psum x1, blocking collectives: 279 us -> 43.9 us  [shards(): packed = lax.psum(packed, ('replica', 'shard'))]
    reduce_scatter x5 -> x0, waiting for transfers between devices: 184 us -> none  [the longest x1 50.4 us: shards(): lax.psum_scatter(grad_down.astype(jnp.bfloat16), 'shard', scatter_dimensi...]
    dot_general x98 -> x0, matrix products: 170 us -> none  [the longest x12 22.5 us: block_backward(): jnp.dot(score_grad, key_head, preferred_element_type=f32) * score_scale]
    ppermute x0 -> x56, waiting for transfers between devices: none -> 99.1 us  [the longest x4 42.6 us: gather_rows(): by_row = lax.ppermute(block, 'shard', ROWY)]
    ppermute x0 -> x56, starting transfers between devices: none -> 68 us  [the longest x12 27.4 us: plane_gather(): got = lax.ppermute(value, 'replica', pairs)]
    all_gather x5 -> x0, waiting for transfers between devices: 58 us -> none  [the longest x1 25.3 us: shards(): kv_all = lax.all_gather(kv_own, 'shard', axis=0, tiled=True)]
    pallas_call x0 -> x7, Pallas kernels: none -> 57.4 us  [call(): pl.pallas_call(body, out_shape=[jax.ShapeDtypeStruct(s, d) for s, d in ou...]
    unnamed x2 -> x0, blocking collectives: 23 us -> none
  transfers between devices with their start and end apart: 11 -> 56, of which waited for: 9 -> 24; matrix products, arithmetic and copies ran while one was open for 14% -> 14% of each run, Pallas kernels for 0% -> 8%
where the time goes in v1:
time: 344 us; the launch traced here: 340 us
  waiting for transfers between devices  99.1 us (29%)
  starting transfers between devices  68 us (20%)
  Pallas kernels  57.4 us (17%)
  local copies, waits for them, and re-layouts  48.6 us (14%)
  blocking collectives  43.9 us (13%)
  other arithmetic  21 us (6%)
    pallas_call x7, Pallas kernels, call(): pl.pallas_call(body, out_shape=[jax.ShapeDtypeStruct(s, d) for s, d in ou...  57.4 us
    psum x1, blocking collectives, shards(): packed = lax.psum(packed, ('replica', 'shard'))  43.9 us
    ppermute x4, waiting for transfers between devices, gather_rows(): by_row = lax.ppermute(block, 'shard', ROWY)  42.6 us
    ppermute x12, waiting for transfers between devices, plane_scatter(): got = lax.ppermute(send.astype(bf16), 'replica', pairs)  30.2 us
    ppermute x12, starting transfers between devices, plane_gather(): got = lax.ppermute(value, 'replica', pairs)  27.4 us
    ppermute x12, starting transfers between devices, plane_scatter(): got = lax.ppermute(send.astype(bf16), 'replica', pairs)  22.5 us
    ppermute x12, waiting for transfers between devices, plane_gather(): got = lax.ppermute(value, 'replica', pairs)  11.7 us
    reshape x3, local copies, waits for them, and re-layouts, shards(): final_qkv.reshape(part, 4, 3, part).transpose(0, 2, 1, 3)  9.85 us
  transfers between devices with their start and end apart: 56, of which 24 were waited for; matrix products, arithmetic and copies ran while one was open for 14% of the time, Pallas kernels for 8%

profile of v1, /device:TPU:0, one launch (start us, length us, event | category | flops | bytes accessed | tf_op | source)
XLA Modules:
  0.0 340.0 jit_solution(2825395313447997873)
XLA Ops:
  0.7 2.9 reshape.195
  5.2 3.0 collective-permute-start.4
  10.9 17.5 %collective-permute-done.1.b2 = bf16[272,768]{1,0:T(8,128)(2,1)S(1)} collective-permute-done((bf16[272,768]{1,0:T(8,128)(2,1)S(1)}, bf16[272,768]{1,0:T(8,128)(2,1)S(1)}, u32[]{:S(2)}, u32[]{:S(2)}) %collective-permute-start.1) | collective-permute-done | bytes 417824 | tf_op jit(solution)/shard_map/ppermute | solution.py:255
  32.7 14.4 %shard_map.263 = (bf16[512,768]{1,0:T(8,128)(2,1)}, f32[512,768]{1,0:T(8,128)}, f32[256,768]{1,0:T(8,128)}, f32[16,768]{1,0:T(8,128)}, bf16[1024,576]{1,0:T(8,12...) custom-call(s32[1]{0:T(128)} %bitcast.rank_ref, ...), custom_call_target="tpu_custom_call" | custom-call | tf_op jit(solution)/shard_map/pallas_call | solution.py:346
  57.3 6.4 %collective-permute-done.7.yrecv_ref = bf16[256,768]{1,0:T(8,128)(2,1)S(1)} collective-permute-done((bf16[256,768]{1,0:T(8,128)(2,1)S(1)}, bf16[256,768]{1,0:T(8,128)(2,1)S(1)}, u32[]{:S(2)}, u32[]{:S(2)}) %collective-permute-start.7) | collective-permute-done | bytes 393248 | tf_op jit(solution)/shard_map/ppermute | solution.py:270
  64.5 2.9 shard_map.264
  69.7 15.1 %collective-permute-done.12.c2 = bf16[256,768]{1,0:T(8,128)(2,1)S(1)} collective-permute-done((bf16[256,768]{1,0:T(8,128)(2,1)S(1)}, bf16[256,768]{1,0:T(8,128)(2,1)S(1)}, u32[]{:S(2)}, u32[]{:S(2)}) %collective-permute-start.12) | collective-permute-done | bytes 393248 | tf_op jit(solution)/shard_map/ppermute | solution.py:255
  85.3 7.4 %collective-permute-done.9.n2 = bf16[256,768]{1,0:T(8,128)(2,1)S(1)} collective-permute-done((bf16[256,768]{1,0:T(8,128)(2,1)}, bf16[256,768]{1,0:T(8,128)(2,1)S(1)}, u32[]{:S(2)}, u32[]{:S(2)}) %collective-permute-start.9) | collective-permute-done | bytes 393248 | tf_op jit(solution)/shard_map/ppermute | solution.py:255
  98.2 8.7 %shard_map.265 = (bf16[512,768]{1,0:T(8,128)(2,1)}, f32[512,768]{1,0:T(8,128)}, bf16[1024,768]{1,0:T(8,128)(2,1)}, bf16[1024,768]{1,0:T(8,128)(2,1)}) custom-call(s32[1]{0:T(128)} %bitcast.rank_ref, bf16[256,768]{1,0:T(8,128)(2,1)} %get-tuple-element.49.n0, bf16[256,768]{1,0:T(8,128)(2,1)} %copy-done.7, bf16[256,768]{1,0:T(8,128)(2,1)} %copy-done.4, ...), custom_call_target="tpu_custom_call" | custom-call | tf_op jit(solution)/shard_map/pallas_call | solution.py:346
  106.9 8.5 %shard_map.266 = (bf16[512,768]{1,0:T(8,128)(2,1)}, f32[512,768]{1,0:T(8,128)}, bf16[768,768]{1,0:T(8,128)(2,1)}, bf16[768,768]{1,0:T(8,128)(2,1)}, f32[8,768]{1,0:T(8,128)}) custom-call(bf16[256,768]{1,0:T(8,128)(2,1)} %get-tuple-element.49.n0, bf16[256,768]{1,0:T(8,128)(2,1)} %copy-done.7, bf16[256,768]{1,0:T(8,128)(2,1)} %copy-done.4, ...), custom_call_target="tpu_custom_call" | custom-call | tf_op jit(solution)/shard_map/pallas_call | solution.py:346
  123.7 8.6 %collective-permute-done.41 = bf16[4,4,24,768]{3,2,1,0:T(8,128)(2,1)S(1)} collective-permute-done((bf16[4,4,24,768]{3,2,1,0:T(8,128)(2,1)S(1)}, bf16[4,4,24,768]{3,2,1,0:T(8,128)(2,1)S(1)}, u32[]{:S(2)}, u32[]{:S(2)}) %collective-permute-start.41) | collective-permute-done | bytes 589856 | tf_op jit(solution)/shard_map/ppermute | solution.py:297
  132.5 3.8 %collective-permute-start.42 = (bf16[2,4,24,768]{3,2,1,0:T(8,128)(2,1)S(1)}, bf16[2,4,24,768]{3,2,1,0:T(8,128)(2,1)S(1)}, u32[]{:S(2)}, u32[]{:S(2)}) collective-permute-start(bf16[2,4,24,768]{3,2,1,0:T(8,128)(2,1)S(1)} %fusion), channel_id=1, source_target_pairs={{0,24},{4,28},{8,16},{12,20},{16,8},{20,12},{24,0},{28,4},{1,25},{... | collective-permute-start | bytes 884744 | tf_op jit(solution)/shard_map/ppermute | solution.py:297
  152.0 3.7 %collective-permute-start.52 = (bf16[1,96,768]{2,1,0:T(8,128)(2,1)S(1)}, bf16[1,96,768]{2,1,0:T(8,128)(2,1)S(1)}, u32[]{:S(2)}, u32[]{:S(2)}) collective-permute-start(bf16[1,96,768]{2,1,0:T(8,128)(2,1)S(1)} %dynamic-slice_convert_fusion.3), channel_id=1, source_target_pairs={{0,24},{4,28},{8,16},{12,20},{16,8},{20,12},{24,0},{28,4},{1,25},{... | collective-permute-start | bytes 442376 | tf_op jit(solution)/shard_map/ppermute | solution.py:297
  155.6 3.4 collective-permute-done.45
  159.1 3.7 %collective-permute-start.53 = (bf16[1,96,768]{2,1,0:T(8,128)(2,1)S(1)}, bf16[1,96,768]{2,1,0:T(8,128)(2,1)S(1)}, u32[]{:S(2)}, u32[]{:S(2)}) collective-permute-start(bf16[1,96,768]{2,1,0:T(8,128)(2,1)S(1)} %add_convert_fusion.5), channel_id=1, source_target_pairs={{0,24},{4,28},{8,16},{12,20},{16,8},{20,12},{24,0},{28,4},{1,25},{... | collective-permute-start | bytes 442376 | tf_op jit(solution)/shard_map/ppermute | solution.py:308
  168.2 3.3 collective-permute-start.54
  172.2 3.6 %shard_map.267 = (f32[256,768]{1,0:T(8,128)}, bf16[256,768]{1,0:T(8,128)(2,1)}, f32[8,768]{1,0:T(8,128)}) custom-call(f32[256,768]{1,0:T(8,128)} %get-tuple-element.48.mid_ref, f32[16,768]{1,0:T(8,128)} %get-tuple-element.45.par_ref, bf16[256,768]{1,0:T(8,128)(2,1)} %cot_ref.1, f32[256,768]{1,0:T(8,128)} %get-tuple-element.77.keep_ref, ...), custom_call_target="tpu_custom_call" | custom-call | tf_op jit(solution)/shard_map/pallas_call | solution.py:346
  193.4 4.6 %collective-permute-start.49 = (bf16[4,4,24,768]{3,2,1,0:T(8,128)(2,1)}, bf16[4,4,24,768]{3,2,1,0:T(8,128)(2,1)S(1)}, u32[]{:S(2)}, u32[]{:S(2)}) collective-permute-start(bf16[4,4,24,768]{3,2,1,0:T(8,128)(2,1)} %pad_maximum_fusion.2), channel_id=1, source_target_pairs={{0,8},{4,12},{8,0},{12,4},{16,24},{20,28},{24,16},{28,20},{1,9},{5... | collective-permute-start | bytes 1769480 | tf_op jit(solution)/shard_map/ppermute | solution.py:308
  198.9 15.6 %shard_map.268 = (bf16[512,768]{1,0:T(8,128)(2,1)}, f32[512,768]{1,0:T(8,128)}, bf16[192,768]{1,0:T(8,128)(2,1)}, bf16[768,576]{1,0:T(8,128)(2,1)}, f32[8,768]{1,0:T(8,128)}) custom-call(s32[1]{0:T(128)} %bitcast.rank_ref, s32[1024,1]{1,0:T(8,128)} %copy.82.segc_ref, s32[1,1024]{1,0:T(1,128)} %bitcast.174, bf16[256,768]{1,0:T(8,128)(2,1)} %get-tuple-element.57.g0, ...), custom_call_target="tpu_custom_call" | custom-call | tf_op jit(solution)/shard_map/pallas_call | solution.py:346
  220.3 2.7 collective-permute-start.35
  223.2 5.0 %collective-permute-done.35 = bf16[4,24,768]{2,1,0:T(8,128)(2,1)S(1)} collective-permute-done((bf16[4,24,768]{2,1,0:T(8,128)(2,1)S(1)}, bf16[4,24,768]{2,1,0:T(8,128)(2,1)S(1)}, u32[]{:S(2)}, u32[]{:S(2)}) %collective-permute-start.35) | collective-permute-done | bytes 147488 | tf_op jit(solution)/shard_map/ppermute | solution.py:297
  234.2 3.0 collective-permute-done.37
  245.7 3.6 %collective-permute-done.27 = bf16[2,4,24,576]{3,2,1,0:T(8,128)(2,1)S(1)} collective-permute-done((bf16[2,4,24,576]{3,2,1,0:T(8,128)(2,1)S(1)}, bf16[2,4,24,576]{3,2,1,0:T(8,128)(2,1)S(1)}, u32[]{:S(2)}, u32[]{:S(2)}) %collective-permute-start.27) | collective-permute-done | bytes 221216 | tf_op jit(solution)/shard_map/ppermute | solution.py:297
  249.4 2.7 collective-permute-start.28
  253.3 2.9 collective-permute-done.28
  266.1 3.1 collective-permute-done.32
  269.3 3.2 collective-permute-start.33
  277.3 3.7 %shard_map.269 = (bf16[256,768]{1,0:T(8,128)(2,1)}, f32[8,768]{1,0:T(8,128)}) custom-call(f32[256,768]{1,0:T(8,128)} %get-tuple-element.44.sin_ref, f32[16,768]{1,0:T(8,128)} %get-tuple-element.45.par_ref, bf16[272,768]{1,0:T(8,128)(2,1)} %copy-done, f32[256,768]{1,0:T(8,128)} %get-tuple-element.56.grad_ref, f32[256,768]{1,0:T(8,128)} %get-tuple-element.75.keep_ref, ...), custom_call_target="tpu_custom_call" | custom-call | tf_op jit(solution)/shard_map/pallas_call | solution.py:346
  282.6 43.9 %psum.7 = f32[15,4,192]{2,0,1:T(8,128)S(1)} all-reduce(f32[15,4,192]{2,0,1:T(8,128)S(1)} %pad_maximum_fusion.15), channel_id=1, replica_groups=mesh['replica'=8,'shard'=4] {'replica','shard'}, use_global_device_ids=true, to_apply=%region_0.1 | all-reduce | flops 11520 | bytes 92160 | tf_op jit(solution)/shard_map/psum | solution.py:422
  330.0 3.3 reshape.224
  333.2 2.9 copy.92
  336.1 3.7 %reshape.215 = f32[192,2304]{1,0:T(8,128)} reshape(f32[192,3,4,192]{3,2,1,0:T(4,128)} %copy.92) | data formatting | bytes 3538944 | tf_op jit(solution)/shard_map/reshape | solution.py:414
  (317 shorter events, 117.2 us)
Async XLA Ops:
  5.2 23.2 %collective-permute-start.4 = (bf16[2,192,576]{2,1,0:T(8,128)(2,1)S(1)}, bf16[2,192,576]{2,1,0:T(8,128)(2,1)S(1)}, u32[]{:S(2)}, u32[]{:S(2)}) collective-permute-start(bf16[2,192,576]{2,1,0:T(8,128)(2,1)S(1)} %pad_maximum_fusion.4), channel_id=1, source_target_pairs={{0,2},{1,3},{2,0},{3,1},{4,6},{5,7},{6,4},{7,5},{8,10},{9,11},{10,... | collective-permute-start | bytes 1327112 | tf_op jit(solution)/shard_map/ppermute | solution.py:261
  9.3 19.1 %collective-permute-start.1 = (bf16[272,768]{1,0:T(8,128)(2,1)S(1)}, bf16[272,768]{1,0:T(8,128)(2,1)S(1)}, u32[]{:S(2)}, u32[]{:S(2)}) collective-permute-start(bf16[272,768]{1,0:T(8,128)(2,1)S(1)} %concatenate.42.b0.ids_ref), channel_id=1, source_target_pairs={{0,2},{1,3},{2,0},{3,1},{4,6},{5,7},{6,4},{7,5},{8,10},{9,11},{10,... | collective-permute-start | bytes 1253384 | tf_op jit(solution)/shard_map/ppermute | solution.py:255
  9.6 22.1 %collective-permute-start = (bf16[272,768]{1,0:T(8,128)(2,1)S(1)}, bf16[272,768]{1,0:T(8,128)(2,1)S(1)}, u32[]{:S(2)}, u32[]{:S(2)}) collective-permute-start(bf16[272,768]{1,0:T(8,128)(2,1)S(1)} %concatenate.42.b0.ids_ref), channel_id=1, source_target_pairs={{0,1},{1,0},{2,3},{3,2},{4,5},{5,4},{6,7},{7,6},{8,9},{9,8},{10,11... | collective-permute-start | bytes 1253384 | tf_op jit(solution)/shard_map/ppermute | solution.py:254
  10.4 21.2 %collective-permute-start.3 = (bf16[192,576]{1,0:T(8,128)(2,1)}, bf16[192,576]{1,0:T(8,128)(2,1)S(1)}, u32[]{:S(2)}, u32[]{:S(2)}) collective-permute-start(bf16[192,576]{1,0:T(8,128)(2,1)} %bitcast.172), channel_id=1, source_target_pairs={{0,1},{1,0},{2,3},{3,2},{4,5},{5,4},{6,7},{7,6},{8,9},{9,8},{10,11... | collective-permute-start | bytes 663560 | tf_op jit(solution)/shard_map/ppermute | solution.py:262
  51.8 11.9 %collective-permute-start.7 = (bf16[256,768]{1,0:T(8,128)(2,1)S(1)}, bf16[256,768]{1,0:T(8,128)(2,1)S(1)}, u32[]{:S(2)}, u32[]{:S(2)}) collective-permute-start(bf16[256,768]{1,0:T(8,128)(2,1)S(1)} %get-tuple-element.78), channel_id=1, source_target_pairs={{0,2},{1,3},{2,0},{3,1},{4,6},{5,7},{6,4},{7,5},{8,10},{9,11},{10,... | collective-permute-start | bytes 1179656 | tf_op jit(solution)/shard_map/ppermute | solution.py:270
  54.5 30.3 %collective-permute-start.15 = (bf16[2,192,768]{2,1,0:T(8,128)(2,1)}, bf16[2,192,768]{2,1,0:T(8,128)(2,1)}, u32[]{:S(2)}, u32[]{:S(2)}) collective-permute-start(bf16[2,192,768]{2,1,0:T(8,128)(2,1)} %pad_maximum_fusion.1), channel_id=1, source_target_pairs={{0,2},{1,3},{2,0},{3,1},{4,6},{5,7},{6,4},{7,5},{8,10},{9,11},{10,... | collective-permute-start | bytes 1769480 | tf_op jit(solution)/shard_map/ppermute | solution.py:261
  54.8 30.0 %collective-permute-start.12 = (bf16[256,768]{1,0:T(8,128)(2,1)S(1)}, bf16[256,768]{1,0:T(8,128)(2,1)S(1)}, u32[]{:S(2)}, u32[]{:S(2)}) collective-permute-start(bf16[256,768]{1,0:T(8,128)(2,1)S(1)} %copy-done.1), channel_id=1, source_target_pairs={{0,2},{1,3},{2,0},{3,1},{4,6},{5,7},{6,4},{7,5},{8,10},{9,11},{10,... | collective-permute-start | bytes 1179656 | tf_op jit(solution)/shard_map/ppermute | solution.py:255
  67.3 25.4 %collective-permute-start.9 = (bf16[256,768]{1,0:T(8,128)(2,1)}, bf16[256,768]{1,0:T(8,128)(2,1)S(1)}, u32[]{:S(2)}, u32[]{:S(2)}) collective-permute-start(bf16[256,768]{1,0:T(8,128)(2,1)} %get-tuple-element.49.n0), channel_id=1, source_target_pairs={{0,2},{1,3},{2,0},{3,1},{4,6},{5,7},{6,4},{7,5},{8,10},{9,11},{10,... | collective-permute-start | bytes 1179656 | tf_op jit(solution)/shard_map/ppermute | solution.py:255
  69.1 25.7 %collective-permute-start.14 = (bf16[192,768]{1,0:T(8,128)(2,1)S(1)}, bf16[192,768]{1,0:T(8,128)(2,1)}, u32[]{:S(2)}, u32[]{:S(2)}) collective-permute-start(bf16[192,768]{1,0:T(8,128)(2,1)S(1)} %bitcast.169), channel_id=1, source_target_pairs={{0,1},{1,0},{2,3},{3,2},{4,5},{5,4},{6,7},{7,6},{8,9},{9,8},{10,11... | collective-permute-start | bytes 884744 | tf_op jit(solution)/shard_map/ppermute | solution.py:262
  69.2 27.8 %collective-permute-start.11 = (bf16[256,768]{1,0:T(8,128)(2,1)S(1)}, bf16[256,768]{1,0:T(8,128)(2,1)S(1)}, u32[]{:S(2)}, u32[]{:S(2)}) collective-permute-start(bf16[256,768]{1,0:T(8,128)(2,1)S(1)} %copy-done.1), channel_id=1, source_target_pairs={{0,1},{1,0},{2,3},{3,2},{4,5},{5,4},{6,7},{7,6},{8,9},{9,8},{10,11... | collective-permute-start | bytes 1179656 | tf_op jit(solution)/shard_map/ppermute | solution.py:254
  84.8 12.2 %collective-permute-start.13 = (bf16[256,768]{1,0:T(8,128)(2,1)S(1)}, bf16[256,768]{1,0:T(8,128)(2,1)S(1)}, u32[]{:S(2)}, u32[]{:S(2)}) collective-permute-start(bf16[256,768]{1,0:T(8,128)(2,1)S(1)} %collective-permute-done.12.c2), channel_id=1, source_target_pairs={{0,1},{1,0},{2,3},{3,2},{4,5},{5,4},{6,7},{7,6},{8,9},{9,8},{10,11... | collective-permute-start | bytes 1179656 | tf_op jit(solution)/shard_map/ppermute | solution.py:256
  84.8 12.2 %collective-permute-start.8 = (bf16[256,768]{1,0:T(8,128)(2,1)}, bf16[256,768]{1,0:T(8,128)(2,1)S(1)}, u32[]{:S(2)}, u32[]{:S(2)}) collective-permute-start(bf16[256,768]{1,0:T(8,128)(2,1)} %get-tuple-element.49.n0), channel_id=1, source_target_pairs={{0,1},{1,0},{2,3},{3,2},{4,5},{5,4},{6,7},{7,6},{8,9},{9,8},{10,11... | collective-permute-start | bytes 1179656 | tf_op jit(solution)/shard_map/ppermute | solution.py:254
  116.8 15.5 %collective-permute-start.41 = (bf16[4,4,24,768]{3,2,1,0:T(8,128)(2,1)S(1)}, bf16[4,4,24,768]{3,2,1,0:T(8,128)(2,1)S(1)}, u32[]{:S(2)}, u32[]{:S(2)}) collective-permute-start(bf16[4,4,24,768]{3,2,1,0:T(8,128)(2,1)S(1)} %bitcast.168), channel_id=1, source_target_pairs={{0,8},{4,12},{8,0},{12,4},{16,24},{20,28},{24,16},{28,20},{1,9},{5... | collective-permute-start | bytes 1769480 | tf_op jit(solution)/shard_map/ppermute | solution.py:297
  120.0 17.8 %collective-permute-start.17 = (bf16[512,768]{1,0:T(8,128)(2,1)}, bf16[512,768]{1,0:T(8,128)(2,1)}, u32[]{:S(2)}, u32[]{:S(2)}) collective-permute-start(bf16[512,768]{1,0:T(8,128)(2,1)} %get-tuple-element.53), channel_id=1, source_target_pairs={{0,1},{1,0},{2,3},{3,2},{4,5},{5,4},{6,7},{7,6},{8,9},{9,8},{10,11... | collective-permute-start | bytes 2359304 | tf_op jit(solution)/shard_map/ppermute | solution.py:268
  120.0 20.7 %collective-permute-start.19 = (bf16[512,768]{1,0:T(8,128)(2,1)}, bf16[512,768]{1,0:T(8,128)(2,1)}, u32[]{:S(2)}, u32[]{:S(2)}) collective-permute-start(bf16[512,768]{1,0:T(8,128)(2,1)} %get-tuple-element.55), channel_id=1, source_target_pairs={{0,1},{1,0},{2,3},{3,2},{4,5},{5,4},{6,7},{7,6},{8,9},{9,8},{10,11... | collective-permute-start | bytes 2359304 | tf_op jit(solution)/shard_map/ppermute | solution.py:268
  122.0 15.3 %collective-permute-start.50 = (bf16[4,96,768]{2,1,0:T(8,128)(2,1)S(1)}, bf16[4,96,768]{2,1,0:T(8,128)(2,1)S(1)}, u32[]{:S(2)}, u32[]{:S(2)}) collective-permute-start(bf16[4,96,768]{2,1,0:T(8,128)(2,1)S(1)} %dynamic-slice_bitcast_fusion), channel_id=1, source_target_pairs={{0,4},{4,0},{8,12},{12,8},{16,20},{20,16},{24,28},{28,24},{1,5},{5... | collective-permute-start | bytes 1769480 | tf_op jit(solution)/shard_map/ppermute | solution.py:297
  132.5 12.4 %collective-permute-start.42 = (bf16[2,4,24,768]{3,2,1,0:T(8,128)(2,1)S(1)}, bf16[2,4,24,768]{3,2,1,0:T(8,128)(2,1)S(1)}, u32[]{:S(2)}, u32[]{:S(2)}) collective-permute-start(bf16[2,4,24,768]{3,2,1,0:T(8,128)(2,1)S(1)} %fusion), channel_id=1, source_target_pairs={{0,24},{4,28},{8,16},{12,20},{16,8},{20,12},{24,0},{28,4},{1,25},{... | collective-permute-start | bytes 884744 | tf_op jit(solution)/shard_map/ppermute | solution.py:297
  137.5 11.7 %collective-permute-start.51 = (bf16[2,96,768]{2,1,0:T(8,128)(2,1)S(1)}, bf16[2,96,768]{2,1,0:T(8,128)(2,1)S(1)}, u32[]{:S(2)}, u32[]{:S(2)}) collective-permute-start(bf16[2,96,768]{2,1,0:T(8,128)(2,1)S(1)} %fusion.1), channel_id=1, source_target_pairs={{0,8},{4,12},{8,0},{12,4},{16,24},{20,28},{24,16},{28,20},{1,9},{5... | collective-permute-start | bytes 884744 | tf_op jit(solution)/shard_map/ppermute | solution.py:297
  139.0 39.2 %collective-permute-start.18 = (bf16[256,768]{1,0:T(8,128)(2,1)S(1)}, bf16[256,768]{1,0:T(8,128)(2,1)}, u32[]{:S(2)}, u32[]{:S(2)}) collective-permute-start(bf16[256,768]{1,0:T(8,128)(2,1)S(1)} %add_convert_fusion.3), channel_id=1, source_target_pairs={{0,2},{1,3},{2,0},{3,1},{4,6},{5,7},{6,4},{7,5},{8,10},{9,11},{10,... | collective-permute-start | bytes 1179656 | tf_op jit(solution)/shard_map/ppermute | solution.py:270
  142.7 28.8 %collective-permute-start.20 = (bf16[256,768]{1,0:T(8,128)(2,1)S(1)}, bf16[256,768]{1,0:T(8,128)(2,1)S(1)}, u32[]{:S(2)}, u32[]{:S(2)}) collective-permute-start(bf16[256,768]{1,0:T(8,128)(2,1)S(1)} %get-tuple-element.76), channel_id=1, source_target_pairs={{0,2},{1,3},{2,0},{3,1},{4,6},{5,7},{6,4},{7,5},{8,10},{9,11},{10,... | collective-permute-start | bytes 1179656 | tf_op jit(solution)/shard_map/ppermute | solution.py:270
  163.6 16.7 %collective-permute-start.47 = (bf16[1,4,24,768]{3,2,1,0:T(8,128)(2,1)}, bf16[1,4,24,768]{3,2,1,0:T(8,128)(2,1)}, u32[]{:S(2)}, u32[]{:S(2)}) collective-permute-start(bf16[1,4,24,768]{3,2,1,0:T(8,128)(2,1)} %maximum_bitcast_fusion), channel_id=1, source_target_pairs={{0,4},{4,0},{8,12},{12,8},{16,20},{20,16},{24,28},{28,24},{1,5},{5... | collective-permute-start | bytes 442376 | tf_op jit(solution)/shard_map/ppermute | solution.py:308
  168.2 15.8 %collective-permute-start.54 = (bf16[2,96,768]{2,1,0:T(8,128)(2,1)}, bf16[2,96,768]{2,1,0:T(8,128)(2,1)}, u32[]{:S(2)}, u32[]{:S(2)}) collective-permute-start(bf16[2,96,768]{2,1,0:T(8,128)(2,1)} %pad_maximum_fusion.8), channel_id=1, source_target_pairs={{0,8},{4,12},{8,0},{12,4},{16,24},{20,28},{24,16},{28,20},{1,9},{5... | collective-permute-start | bytes 884744 | tf_op jit(solution)/shard_map/ppermute | solution.py:308
  175.8 22.2 %collective-permute-start.21 = (bf16[256,768]{1,0:T(8,128)(2,1)}, bf16[256,768]{1,0:T(8,128)(2,1)S(1)}, u32[]{:S(2)}, u32[]{:S(2)}) collective-permute-start(bf16[256,768]{1,0:T(8,128)(2,1)} %get-tuple-element.57.g0), channel_id=1, source_target_pairs={{0,1},{1,0},{2,3},{3,2},{4,5},{5,4},{6,7},{7,6},{8,9},{9,8},{10,11... | collective-permute-start | bytes 1179656 | tf_op jit(solution)/shard_map/ppermute | solution.py:254
  175.8 11.8 %collective-permute-start.22 = (bf16[256,768]{1,0:T(8,128)(2,1)}, bf16[256,768]{1,0:T(8,128)(2,1)}, u32[]{:S(2)}, u32[]{:S(2)}) collective-permute-start(bf16[256,768]{1,0:T(8,128)(2,1)} %get-tuple-element.57.g0), channel_id=1, source_target_pairs={{0,2},{1,3},{2,0},{3,1},{4,6},{5,7},{6,4},{7,5},{8,10},{9,11},{10,... | collective-permute-start | bytes 1179656 | tf_op jit(solution)/shard_map/ppermute | solution.py:255
  181.3 11.1 %collective-permute-start.48 = (bf16[2,4,24,768]{3,2,1,0:T(8,128)(2,1)S(1)}, bf16[2,4,24,768]{3,2,1,0:T(8,128)(2,1)S(1)}, u32[]{:S(2)}, u32[]{:S(2)}) collective-permute-start(bf16[2,4,24,768]{3,2,1,0:T(8,128)(2,1)S(1)} %pad_maximum_fusion.7), channel_id=1, source_target_pairs={{0,24},{4,28},{8,16},{12,20},{16,8},{20,12},{24,0},{28,4},{1,25},{... | collective-permute-start | bytes 884744 | tf_op jit(solution)/shard_map/ppermute | solution.py:308
  188.5 34.5 %collective-permute-start.55 = (bf16[4,96,768]{2,1,0:T(8,128)(2,1)}, bf16[4,96,768]{2,1,0:T(8,128)(2,1)S(1)}, u32[]{:S(2)}, u32[]{:S(2)}) collective-permute-start(bf16[4,96,768]{2,1,0:T(8,128)(2,1)} %pad_maximum_fusion.3), channel_id=1, source_target_pairs={{0,4},{4,0},{8,12},{12,8},{16,20},{20,16},{24,28},{28,24},{1,5},{5... | collective-permute-start | bytes 1769480 | tf_op jit(solution)/shard_map/ppermute | solution.py:308
  193.4 40.7 %collective-permute-start.49 = (bf16[4,4,24,768]{3,2,1,0:T(8,128)(2,1)}, bf16[4,4,24,768]{3,2,1,0:T(8,128)(2,1)S(1)}, u32[]{:S(2)}, u32[]{:S(2)}) collective-permute-start(bf16[4,4,24,768]{3,2,1,0:T(8,128)(2,1)} %pad_maximum_fusion.2), channel_id=1, source_target_pairs={{0,8},{4,12},{8,0},{12,4},{16,24},{20,28},{24,16},{28,20},{1,9},{5... | collective-permute-start | bytes 1769480 | tf_op jit(solution)/shard_map/ppermute | solution.py:308
  214.5 50.1 %collective-permute-start.24 = (bf16[512,768]{1,0:T(8,128)(2,1)}, bf16[512,768]{1,0:T(8,128)(2,1)S(1)}, u32[]{:S(2)}, u32[]{:S(2)}) collective-permute-start(bf16[512,768]{1,0:T(8,128)(2,1)} %get-tuple-element.64), channel_id=1, source_target_pairs={{0,1},{1,0},{2,3},{3,2},{4,5},{5,4},{6,7},{7,6},{8,9},{9,8},{10,11... | collective-permute-start | bytes 2359304 | tf_op jit(solution)/shard_map/ppermute | solution.py:268
  217.8 25.0 %collective-permute-start.26 = (bf16[4,4,24,576]{3,2,0,1:T(8,128)(2,1)S(1)}, bf16[4,4,24,576]{3,2,0,1:T(8,128)(2,1)S(1)}, u32[]{:S(2)}, u32[]{:S(2)}) collective-permute-start(bf16[4,4,24,576]{3,2,0,1:T(8,128)(2,1)S(1)} %dynamic-slice_bitcast_fusion.1), channel_id=1, source_target_pairs={{0,4},{4,0},{8,12},{12,8},{16,20},{20,16},{24,28},{28,24},{1,5},{5... | collective-permute-start | bytes 1327112 | tf_op jit(solution)/shard_map/ppermute | solution.py:297
  265.6 10.9 %collective-permute-start.25 = (bf16[256,768]{1,0:T(8,128)(2,1)S(1)}, bf16[256,768]{1,0:T(8,128)(2,1)S(1)}, u32[]{:S(2)}, u32[]{:S(2)}) collective-permute-start(bf16[256,768]{1,0:T(8,128)(2,1)S(1)} %get-tuple-element.74), channel_id=1, source_target_pairs={{0,2},{1,3},{2,0},{3,1},{4,6},{5,7},{6,4},{7,5},{8,10},{9,11},{10,... | collective-permute-start | bytes 1179656 | tf_op jit(solution)/shard_map/ppermute | solution.py:270
  269.3 12.5 %collective-permute-start.33 = (bf16[2,4,24,576]{3,2,0,1:T(8,128)(2,1)S(1)}, bf16[2,4,24,576]{3,2,0,1:T(8,128)(2,1)S(1)}, u32[]{:S(2)}, u32[]{:S(2)}) collective-permute-start(bf16[2,4,24,576]{3,2,0,1:T(8,128)(2,1)S(1)} %pad_maximum_fusion.9), channel_id=1, source_target_pairs={{0,8},{4,12},{8,0},{12,4},{16,24},{20,28},{24,16},{28,20},{1,9},{5... | collective-permute-start | bytes 663560 | tf_op jit(solution)/shard_map/ppermute | solution.py:308
  282.0 46.4 %collective-permute-start.34 = (bf16[4,4,24,576]{3,2,0,1:T(8,128)(2,1)S(1)}, bf16[4,4,24,576]{3,2,0,1:T(8,128)(2,1)S(1)}, u32[]{:S(2)}, u32[]{:S(2)}) collective-permute-start(bf16[4,4,24,576]{3,2,0,1:T(8,128)(2,1)S(1)} %pad_maximum_fusion.5), channel_id=1, source_target_pairs={{0,4},{4,0},{8,12},{12,8},{16,20},{20,16},{24,28},{28,24},{1,5},{5... | collective-permute-start | bytes 1327112 | tf_op jit(solution)/shard_map/ppermute | solution.py:308
  (72 other events, 342.7 us)
